TPU v7x, 32 devices: a whole 2x2x4 slice. The times are simulated.
32 devices in a mesh: dp: 4 (over z), seq: 8 (over y, x, core).
Axes of the slice: x: 2, y: 2, z: 4, core: 2. Of those that a mesh axis runs over, the one named last changes fastest.
Arguments:
- tiles: bfloat16 [4, 1536, 768], P('dp', 'seq'), may hold values from -40 to 40
- cotangent: bfloat16 [4, 1536, 768], P('dp', 'seq'), may hold values from -0.078125 to 0.078125
- segment_of: int32 [4, 1536, 1], P('dp', 'seq'), may hold values from 0 to 15; in each aligned block of 192 rows (0 to 191, 192 to 383, ..., all dimensions but the last counted through in order) at most 20 rows name the same one
- tissue_count: int32 [4], P('dp'), may hold values from 768 to 1536
- w_query: bfloat16 [768, 768], P('seq'), may hold values from -0.21875 to 0.21875
- w_key: bfloat16 [768, 768], P('seq'), may hold values from -0.21875 to 0.21875
- w_value: bfloat16 [768, 768], P('seq'), may hold values from -0.21875 to 0.21875
- w_out: bfloat16 [768, 768], P('seq'), may hold values from -2.390625 to 2.390625
Outputs:
- layer_out: bfloat16 [4, 1536, 768], P('dp', 'seq')
- grad_value: float32 [768, 768], P('seq')
Inputs may be any that keep to these rules, and one draw needn't show every extreme that they name: `segment_of`: within one slide, the 192 tiles of one block name one group at most 20 times; some group is named exactly 20 times.
All inputs are finite; a program needn't handle non-finite values.
Results may differ from a plain program's by a relative error of at most 0.014.
Values may be sent and summed in bfloat16 or wider, within the bound.
No kernel may reach another device: no remote copies, remote signals or barrier semaphores. Data moves between devices by JAX's collectives and lax.ppermute only.
A program may use at most 64 MiB of HBM per device.

v0:
```python
import jax
import jax.numpy as jnp
from jax import lax
from jax.sharding import PartitionSpec as P

HEADS = 12
SEG_DEV = 2
NEG_BIG = -1e30


def contract_last(left, right):
    return lax.dot_general(
        left, right, (((1,), (1,)), ((), ())), preferred_element_type=jnp.float32
    )


def contract_first(left, right):
    return lax.dot_general(
        left, right, (((0,), (0,)), ((), ())), preferred_element_type=jnp.float32
    )


def local(tiles, cotangent, segment_of, tissue_count, w_query, w_key, w_value, w_out):
    rows = tiles.shape[1]
    width = tiles.shape[2]
    heads = HEADS
    head_dim = width // heads
    scale = head_dim ** (-0.5)
    seq_count = lax.axis_size("seq")
    own_index = lax.axis_index("seq")
    segments = SEG_DEV * seq_count
    capacity = 5 * rows // (3 * segments)
    slots = segments * capacity
    per_segment = seq_count * capacity
    full_query, full_key, full_value, full_out = (
        lax.all_gather(w_query, "seq", axis=0, tiled=True),
        lax.all_gather(w_key, "seq", axis=0, tiled=True),
        lax.all_gather(w_value, "seq", axis=0, tiled=True),
        lax.all_gather(w_out, "seq", axis=0, tiled=True),
    )
    inputs = tiles[0]
    position = own_index * rows + jnp.arange(rows, dtype=jnp.int32)
    inside = position < tissue_count[0]
    masked_cot = cotangent[0] * inside[:, None].astype(jnp.bfloat16)
    query_rows = jnp.dot(inputs, full_query, preferred_element_type=jnp.float32).astype(
        jnp.bfloat16
    )
    key_rows = jnp.dot(inputs, full_key, preferred_element_type=jnp.float32).astype(jnp.bfloat16)
    value_rows = jnp.dot(inputs, full_value, preferred_element_type=jnp.float32).astype(
        jnp.bfloat16
    )
    dout_rows = contract_last(masked_cot, full_out).astype(jnp.bfloat16)

    def by_heads(block):
        return block.reshape(rows, heads, head_dim).transpose(1, 0, 2)

    query_heads = by_heads(query_rows)
    key_heads = by_heads(key_rows)
    visible = inside[None, :] | jnp.eye(rows, dtype=bool)

    def local_scores(query_one, key_one):
        scores = contract_last(query_one, key_one) * scale
        return jnp.where(visible, scores, NEG_BIG)

    def local_stats(pair):
        scores = local_scores(pair[0], pair[1])
        top = jnp.max(scores, axis=1)
        total = jnp.sum(jnp.exp(scores - top[:, None]), axis=1)
        return (top, total)

    local_max, local_sum = lax.map(local_stats, (query_heads, key_heads))
    stats_rows = jnp.stack([local_max.T, local_sum.T], axis=1)
    segment_rows = segment_of[0, :, 0]
    member = (segment_rows[:, None] == jnp.arange(segments, dtype=jnp.int32)[None, :]).astype(
        jnp.int32
    )
    rank = jnp.sum(jnp.cumsum(member, axis=0) * member, axis=1) - 1
    slot_index = segment_rows * capacity + rank
    source_row = (
        jnp.full((slots,), rows, jnp.int32).at[slot_index].set(jnp.arange(rows, dtype=jnp.int32))
    )
    state_rows = jnp.where(inside, 2, 1).astype(jnp.int32)

    def to_slots(block):
        padded = jnp.concatenate([block, jnp.zeros((1,) + block.shape[1:], block.dtype)], axis=0)
        gathered = jnp.take(padded, source_row, axis=0)
        return gathered.reshape((seq_count, SEG_DEV, capacity) + block.shape[1:])

    members = [query_rows, key_rows, value_rows, dout_rows]
    bulk_rows = jnp.stack(members, axis=1)

    def unpack(bulk_one):
        return (bulk_one[:, 0], bulk_one[:, 1], bulk_one[:, 2], bulk_one[:, 3])

    send_bulk = to_slots(bulk_rows)
    send_stats = to_slots(stats_rows)
    send_state = to_slots(state_rows)
    eye_slots = jnp.eye(per_segment, dtype=bool)
    bulk = lax.all_to_all(
        send_bulk.astype(jnp.float32), "seq", split_axis=0, concat_axis=2, tiled=True
    ).astype(send_bulk.dtype)
    stats = lax.all_to_all(send_stats, "seq", split_axis=0, concat_axis=2, tiled=True)
    state = lax.all_to_all(send_state, "seq", split_axis=0, concat_axis=2, tiled=True)

    def one_segment(item):
        bulk_one, stats_one, state_one = item
        query_seg, key_seg, value_seg, dout_seg = unpack(bulk_one)
        slot_count = query_seg.shape[0]
        query_seg = query_seg.reshape(slot_count, heads, head_dim)
        key_seg = key_seg.reshape(slot_count, heads, head_dim)
        value_seg = value_seg.reshape(slot_count, heads, head_dim)
        dout_seg = dout_seg.reshape(slot_count, heads, head_dim)
        seen = (state_one == 2)[None, :] | eye_slots
        scores = (
            jnp.einsum("qhc,khc->hqk", query_seg, key_seg, preferred_element_type=jnp.float32)
            * scale
        )
        scores = jnp.where(seen[None], scores, NEG_BIG)
        far_max = jnp.max(scores, axis=2)
        far_sum = jnp.sum(jnp.exp(scores - far_max[:, :, None]), axis=2)
        seg_near_max = stats_one[:, 0, :].T
        seg_near_sum = stats_one[:, 1, :].T
        top = jnp.maximum(far_max, seg_near_max)
        log_total = top + jnp.log(
            seg_near_sum * jnp.exp(seg_near_max - top) + far_sum * jnp.exp(far_max - top)
        )
        weights = jnp.exp(scores - log_total[:, :, None]).astype(jnp.bfloat16)
        far_out = jnp.einsum("hqk,khc->qhc", weights, value_seg, preferred_element_type=jnp.float32)
        far_grad = jnp.einsum("hqk,qhc->khc", weights, dout_seg, preferred_element_type=jnp.float32)
        far_out = far_out.astype(jnp.bfloat16).reshape(slot_count, width)
        far_grad = far_grad.astype(jnp.bfloat16).reshape(slot_count, width)
        return (far_out, far_grad, log_total.T)

    far_out, far_grad, totals = lax.map(one_segment, (bulk[0], stats[0], state[0]))
    back_bulk = jnp.stack([far_out, far_grad], axis=2)[None]
    back_lse = totals[None]
    home_bulk, home_lse = (
        lax.all_to_all(
            back_bulk.astype(jnp.float32), "seq", split_axis=2, concat_axis=0, tiled=True
        ).astype(back_bulk.dtype),
        lax.all_to_all(back_lse, "seq", split_axis=2, concat_axis=0, tiled=True),
    )
    far_rows = jnp.take(home_bulk.reshape((slots,) + back_bulk.shape[3:]), slot_index, axis=0)
    lse_rows = jnp.take(home_lse.reshape(slots, heads), slot_index, axis=0)

    def local_apply(item):
        query_one, key_one, value_one, dout_one, lse_one = item
        scores = local_scores(query_one, key_one)
        weights = jnp.exp(scores - lse_one[:, None]).astype(jnp.bfloat16)
        near_out = jnp.dot(weights, value_one, preferred_element_type=jnp.float32)
        near_grad = contract_first(weights, dout_one)
        return (near_out, near_grad)

    near_out, near_grad = lax.map(
        local_apply, (query_heads, key_heads, by_heads(value_rows), by_heads(dout_rows), lse_rows.T)
    )
    near_grad = near_grad.transpose(1, 0, 2).reshape(rows, width).astype(jnp.bfloat16)
    far_out_rows = far_rows[:, 0]
    grad_right = far_rows[:, 1]
    attention = (
        near_out.transpose(1, 0, 2).reshape(rows, width) + far_out_rows.astype(jnp.float32)
    ).astype(jnp.bfloat16)
    layer_rows = jnp.dot(attention, full_out, preferred_element_type=jnp.float32).astype(
        jnp.bfloat16
    )
    grad_part = lax.psum_scatter(
        (contract_first(inputs, near_grad) + contract_first(inputs, grad_right)).astype(
            jnp.bfloat16
        ),
        "seq",
        scatter_dimension=0,
        tiled=True,
    ).astype(jnp.float32)
    grad_part = lax.psum(grad_part.astype(jnp.bfloat16), "dp").astype(jnp.float32)
    return (layer_rows[None], grad_part)


def solution(mesh):
    placed = (
        P("dp", "seq", None),
        P("dp", "seq", None),
        P("dp", "seq", None),
        P("dp"),
        P("seq", None),
        P("seq", None),
        P("seq", None),
        P("seq", None),
    )
    return jax.shard_map(
        local,
        mesh=mesh,
        in_specs=placed,
        out_specs=(P("dp", "seq", None), P("seq", None)),
        check_vma=False,
    )
```

profile of v0, /device:TPU:0, one launch (start us, length us, event | category | flops | bytes accessed | tf_op | source)
XLA Modules:
  0.0 328.2 jit_solution(14311517233252371151)
XLA Ops:
  14.5 2.5 gather_fusion.1
  17.6 5.2 %all-to-all-start.1 = ((s32[8,2,20]{2,1,0:T(2,128)}), s32[8,2,20]{2,1,0:T(2,128)S(1)}, u32[]{:S(2)}, u32[]{:S(2)}) async-start(s32[8,2,20]{2,1,0:T(2,128)} %broadcast_select_fusion.2), calls=%async_computation.1 | async-start | bytes 16384 | tf_op jit(solution)/shard_map/all_to_all | solution.py:103
  23.4 13.1 %all-gather.5.cloned.1.call-done = bf16[768,768]{1,0:T(8,128)(2,1)} async-done(((bf16[96,768]{1,0:T(8,128)(2,1)}), bf16[768,768]{1,0:T(8,128)(2,1)}) %all-gather.5.cloned.1.call-update) | async-done | bytes 1179664 | tf_op jit(solution)/shard_map/all_gather | solution.py:36
  36.6 1.7 convolution_convert_fusion.6
  38.7 23.7 %all-gather.7.cloned.1.call-done = bf16[768,768]{1,0:T(8,128)(2,1)} async-done(((bf16[96,768]{1,0:T(8,128)(2,1)}), bf16[768,768]{1,0:T(8,128)(2,1)}) %all-gather.7.cloned.1.call-update) | async-done | bytes 1179664 | tf_op jit(solution)/shard_map/all_gather | solution.py:37
  62.4 1.7 convolution_convert_fusion.5
  64.5 4.9 %while.41 = (s32[]{:T(128)}, f32[12,192]{1,0:T(8,128)S(1)}, f32[12,192]{1,0:T(8,128)S(1)}, bf16[12,192,64]{2,1,0:T(8,128)(2,1)S(1)}, bf16[12,192,64]{2,1,0:T(8,1...) while((s32[]{:T(128)}, f32[12,192]{1,0:T(8,128)S(1)}, ...), condition=%wide.region_7.8_spmd.clone, body=%wide.region_4.7_spmd.clone.sunk | while | flops 4976258 | bytes 400221 | solution.py:71
  70.5 2.0 gather_fusion.2
  73.0 15.2 %all-gather.9.cloned.1.call-done = bf16[768,768]{1,0:T(8,128)(2,1)} async-done(((bf16[96,768]{1,0:T(8,128)(2,1)}), bf16[768,768]{1,0:T(8,128)(2,1)}) %all-gather.9.cloned.1.call-update) | async-done | bytes 1179664 | tf_op jit(solution)/shard_map/all_gather | solution.py:38
  88.2 1.7 convolution_convert_fusion.4
  89.9 24.0 %all-gather.11.cloned.1.call-done = bf16[768,768]{1,0:T(8,128)(2,1)} async-done(((bf16[96,768]{1,0:T(8,128)(2,1)}), bf16[768,768]{1,0:T(8,128)(2,1)}) %all-gather.11.cloned.1.call-update) | async-done | bytes 1179664 | tf_op jit(solution)/shard_map/all_gather | solution.py:39
  113.9 1.8 convolution_convert_fusion.3
  118.9 3.9 %gather_fusion = bf16[320,4,768]{2,1,0:T(4,128)(2,1)S(1)} fusion(bf16[193,4,768]{2,1,0:T(4,128)(2,1)S(1)} %concatenate.16.clone, s32[1024]{0:T(1024)S(1)} %pad_clamp_fusion.1), kind=kCustom, calls=%fused_computation | custom fusion | bytes 3933440 | tf_op jit(solution)/shard_map/jit(_take)/gather | solution.py:86
  122.9 3.3 %all-to-all-start.2 = ((f32[8,1,960]{2,1,0:T(1,128)}), f32[8,1,960]{2,1,0:T(1,128)S(1)}, u32[]{:S(2)}, u32[]{:S(2)}) async-start(f32[8,1,960]{2,1,0:T(1,128)} %reshape.247), calls=%async_computation.2 | async-start | bytes 65536 | tf_op jit(solution)/shard_map/all_to_all | solution.py:102
  126.2 2.1 select_convert_fusion
  128.3 2.6 all-to-all-done.2
  131.0 3.8 %all-to-all-start = ((bf16[8,2,20,4,768]{4,3,2,1,0:T(4,128)(2,1)}), bf16[8,2,20,4,768]{4,3,2,1,0:T(4,128)(2,1)S(1)}, u32[]{:S(2)}, u32[]{:S(2)}) async-start(bf16[8,2,20,4,768]{4,3,2,1,0:T(4,128)(2,1)} %select_convert_fusion), calls=%async_computation | async-start | bytes 3932160 | tf_op jit(solution)/shard_map/all_to_all | solution.py:99
  138.6 21.1 %all-to-all-done = bf16[8,2,20,4,768]{4,3,2,1,0:T(4,128)(2,1)S(1)} async-done(((bf16[8,2,20,4,768]{4,3,2,1,0:T(4,128)(2,1)}), bf16[8,2,20,4,768]{4,3,2,1,0:T(4,128)(2,1)S(1)}, u32[]{:S(2)}, u32[]{:S(2)}) %all-to-all-start) | async-done | bytes 1966112 | tf_op jit(solution)/shard_map/all_to_all | solution.py:99
  159.7 2.0 copy.124
  161.7 11.5 %while.42 = (s32[]{:T(128)}, bf16[2,160,768]{2,1,0:T(8,128)(2,1)}, bf16[2,160,768]{2,1,0:T(8,128)(2,1)}, f32[2,160,12]{1,2,0:T(8,128)S(1)}, bf16[2,160,4,768]{3,...) while((s32[]{:T(128)}, bf16[2,160,768]{2,1,0:T(8,128)(2,1)}, ...), condition=%wide.region_11.12_spmd.clone, body=%wide.region_8.11_spmd.clone.sunk | while | flops 121049760 | bytes 14496293 | solution.py:134
  174.2 3.3 %all-to-all-start.3 = ((f32[8,1,480]{2,1,0:T(1,128)}), f32[8,1,480]{2,1,0:T(1,128)S(1)}, u32[]{:S(2)}, u32[]{:S(2)}) async-start(f32[8,1,480]{2,1,0:T(1,128)} %reshape.249), calls=%async_computation.3 | async-start | bytes 32768 | tf_op jit(solution)/shard_map/all_to_all | solution.py:141
  178.9 2.0 copy.147
  182.3 4.2 %all-to-all-start.4 = ((bf16[1,2,160,2,768]{4,3,1,0,2:T(2,128)(2,1)}), bf16[1,2,160,2,768]{4,3,1,0,2:T(2,128)(2,1)}, u32[]{:S(2)}, u32[]{:S(2)}) async-start(bf16[1,2,160,2,768]{4,3,1,0,2:T(2,128)(2,1)} %copy.147), calls=%async_computation.4 | async-start | bytes 1966080 | tf_op jit(solution)/shard_map/all_to_all | solution.py:138
  189.1 42.2 %while.43 = (s32[]{:T(128)}, f32[12,192,64]{1,2,0:T(8,128)}, bf16[12,192,64]{1,2,0:T(8,128)(2,1)S(1)}, bf16[12,192,64]{2,1,0:T(8,128)(2,1)}, bf16[12,192,64]{2,1...) while((s32[]{:T(128)}, f32[12,192,64]{1,2,0:T(8,128)}, ...), condition=%wide.region_13.14_spmd.clone, body=%wide.region_12.13_spmd.clone.sunk | while | flops 14376962 | bytes 546345 | solution.py:154
  231.9 1.9 copy.148
  233.8 1.6 copy.149
  235.4 3.1 gather_fusion.4
  241.5 2.4 copy.157
  245.4 36.4 %reduce-scatter.4.cloned.1.call-done = bf16[96,768]{1,0:T(8,128)(2,1)} async-done(((bf16[768,768]{1,0:T(8,128)(2,1)}), bf16[96,768]{1,0:T(8,128)(2,1)}) %reduce-scatter.4.cloned.1.call-update) | async-done | bytes 147472
  281.8 1.7 copy.158
  284.7 34.9 %all-reduce.5.cloned.1.call-done = bf16[96,768]{0,1:T(8,128)(2,1)} async-done(((bf16[96,768]{0,1:T(8,128)(2,1)}), bf16[96,768]{0,1:T(8,128)(2,1)}) %all-reduce.5.cloned.1.call-update) | async-done | bytes 147472 | tf_op jit(solution)/shard_map/psum | solution.py:174
  319.6 1.8 copy.151
  (237 shorter events, 87.5 us)
Async XLA Ops:
  7.2 29.4 %copy-start = (bf16[1,192,768]{2,1,0:T(8,128)(2,1)S(1)}, bf16[1,192,768]{2,1,0:T(8,128)(2,1)}, u32[]{:S(2)}) copy-start(bf16[1,192,768]{2,1,0:T(8,128)(2,1)} %param.14) | copy-start | bytes 884740
  7.2 29.4 %all-gather.5.cloned.1.call-start = ((), (), s32[]{:S(2)}) async-start(), calls=%async_computation.6 | async-start | bytes 1327104 | tf_op jit(solution)/shard_map/all_gather | solution.py:36
  7.9 54.5 %all-gather.7.cloned.1.call-start = ((), (), s32[]{:S(2)}) async-start(), calls=%async_computation.7 | async-start | bytes 1327104 | tf_op jit(solution)/shard_map/all_gather | solution.py:37
  8.7 79.6 %all-gather.9.cloned.1.call-start = ((), (), s32[]{:S(2)}) async-start(), calls=%async_computation.8 | async-start | bytes 1327104 | tf_op jit(solution)/shard_map/all_gather | solution.py:38
  17.6 105.2 %all-to-all-start.1 = ((s32[8,2,20]{2,1,0:T(2,128)}), s32[8,2,20]{2,1,0:T(2,128)S(1)}, u32[]{:S(2)}, u32[]{:S(2)}) async-start(s32[8,2,20]{2,1,0:T(2,128)} %broadcast_select_fusion.2), calls=%async_computation.1 | async-start | bytes 16384 | tf_op jit(solution)/shard_map/all_to_all | solution.py:103
  22.8 91.1 %all-gather.11.cloned.1.call-start = ((), (), s32[]{:S(2)}) async-start(), calls=%async_computation.9 | async-start | bytes 1327104 | tf_op jit(solution)/shard_map/all_gather | solution.py:39
  69.4 0.8 copy-start.6
  69.4 3.1 copy-start.7
  70.3 43.6 %copy-start.9 = (bf16[1,192,768]{2,1,0:T(8,128)(2,1)S(1)}, bf16[1,192,768]{2,1,0:T(8,128)(2,1)}, u32[]{:S(2)}) copy-start(bf16[1,192,768]{2,1,0:T(8,128)(2,1)} %param.15) | copy-start | bytes 884740
  89.9 26.7 %copy-start.2 = (bf16[192,768]{1,0:T(8,128)(2,1)}, bf16[192,768]{1,0:T(8,128)(2,1)S(1)}, u32[]{:S(2)}) copy-start(bf16[192,768]{1,0:T(8,128)(2,1)S(1)} %convolution_convert_fusion.4) | copy-start | bytes 884740
  115.7 0.7 copy-start.4
  122.9 8.1 %all-to-all-start.2 = ((f32[8,1,960]{2,1,0:T(1,128)}), f32[8,1,960]{2,1,0:T(1,128)S(1)}, u32[]{:S(2)}, u32[]{:S(2)}) async-start(f32[8,1,960]{2,1,0:T(1,128)} %reshape.247), calls=%async_computation.2 | async-start | bytes 65536 | tf_op jit(solution)/shard_map/all_to_all | solution.py:102
  128.3 6.5 %copy-start.10 = (s32[1,192,1]{1,2,0:T(1,128)S(1)}, s32[1,192,1]{1,2,0:T(1,128)}, u32[]{:S(2)}) copy-start(s32[1,192,1]{1,2,0:T(1,128)} %param.16) | copy-start | bytes 2308
  128.3 6.6 %copy-start.5 = (bf16[192,768]{1,0:T(8,128)(2,1)S(1)}, bf16[192,768]{1,0:T(8,128)(2,1)}, u32[]{:S(2)}) copy-start(bf16[192,768]{1,0:T(8,128)(2,1)} %copy-done.4) | copy-start | bytes 884740
  128.3 7.5 %copy-start.3 = (bf16[192,768]{1,0:T(8,128)(2,1)S(1)}, bf16[192,768]{1,0:T(8,128)(2,1)}, u32[]{:S(2)}) copy-start(bf16[192,768]{1,0:T(8,128)(2,1)} %copy-done.2) | copy-start | bytes 884740
  131.0 28.7 %all-to-all-start = ((bf16[8,2,20,4,768]{4,3,2,1,0:T(4,128)(2,1)}), bf16[8,2,20,4,768]{4,3,2,1,0:T(4,128)(2,1)S(1)}, u32[]{:S(2)}, u32[]{:S(2)}) async-start(bf16[8,2,20,4,768]{4,3,2,1,0:T(4,128)(2,1)} %select_convert_fusion), calls=%async_computation | async-start | bytes 3932160 | tf_op jit(solution)/shard_map/all_to_all | solution.py:99
  174.2 8.0 %all-to-all-start.3 = ((f32[8,1,480]{2,1,0:T(1,128)}), f32[8,1,480]{2,1,0:T(1,128)S(1)}, u32[]{:S(2)}, u32[]{:S(2)}) async-start(f32[8,1,480]{2,1,0:T(1,128)} %reshape.249), calls=%async_computation.3 | async-start | bytes 32768 | tf_op jit(solution)/shard_map/all_to_all | solution.py:141
  180.9 8.3 %copy-start.8 = (bf16[12,192,64]{1,2,0:T(8,128)(2,1)S(1)}, bf16[12,192,64]{1,2,0:T(8,128)(2,1)}, u32[]{:S(2)}) copy-start(bf16[12,192,64]{1,2,0:T(8,128)(2,1)} %custom-call.16) | copy-start | bytes 884740
  182.3 49.6 %all-to-all-start.4 = ((bf16[1,2,160,2,768]{4,3,1,0,2:T(2,128)(2,1)}), bf16[1,2,160,2,768]{4,3,1,0,2:T(2,128)(2,1)}, u32[]{:S(2)}, u32[]{:S(2)}) async-start(bf16[1,2,160,2,768]{4,3,1,0,2:T(2,128)(2,1)} %copy.147), calls=%async_computation.4 | async-start | bytes 1966080 | tf_op jit(solution)/shard_map/all_to_all | solution.py:138
  186.5 95.3 %reduce-scatter.4.cloned.1.call-start = ((), (), s32[]{:S(2)}) async-start(), calls=%async_computation.11 | async-start | bytes 1327104
  243.8 39.7 %copy-start.1 = (bf16[768,768]{1,0:T(8,128)(2,1)S(1)}, bf16[768,768]{1,0:T(8,128)(2,1)}, u32[]{:S(2)}) copy-start(bf16[768,768]{1,0:T(8,128)(2,1)} %all-gather.11.cloned.1.call-done) | copy-start | bytes 3538948
  243.9 75.7 %all-reduce.5.cloned.1.call-start = ((), (), s32[]{:S(2)}) async-start(), calls=%async_computation.10 | async-start | bytes 393216 | tf_op jit(solution)/shard_map/psum | solution.py:174
Sparse Core Ops, SparseCore 0:
  9.9 26.6 all-gather.4
  38.4 23.9 all-gather.6
  64.3 23.9 all-gather.8
  90.0 23.9 all-gather.10
  244.0 37.7 reduce-scatter.3
  284.5 34.9 all-reduce.4
where the time goes:
time: 331 us; the launch traced here: 328 us
  waiting for transfers between devices  175 us (53%)
  matrix products  57.6 us (17%)
  local copies, waits for them, and re-layouts  47.3 us (14%)
  starting transfers between devices  20.3 us (6%)
  between operations  15.3 us (5%)
  other arithmetic  11.8 us (4%)
    unnamed x7, waiting for transfers between devices  39 us
    psum x1, waiting for transfers between devices, local(): lax.psum(grad_part.astype(jnp.bfloat16), 'dp').astype(jnp.float32)  34.9 us
    all_gather x1, waiting for transfers between devices, local(): lax.all_gather(w_out, 'seq', axis=0, tiled=True)  24 us
    all_gather x1, waiting for transfers between devices, local(): lax.all_gather(w_key, 'seq', axis=0, tiled=True)  23.7 us
    all_to_all x1, waiting for transfers between devices, local(): lax.all_to_all(send_bulk.astype(jnp.float32), 'seq', split_axis=0, concat...  21.1 us
    dot_general x12, matrix products, local_apply(): near_out = jnp.dot(weights, value_one, preferred_element_type=jnp.float32)  18.6 us
    dot_general x25, matrix products, contract_last(): lax.dot_general(left, right, (((1,), (1,)), ((), ())), preferred_element_...  17.2 us
    all_gather x1, waiting for transfers between devices, local(): lax.all_gather(w_value, 'seq', axis=0, tiled=True)  15.2 us
  transfers between devices with their start and end apart: 11, of which 9 were waited for; matrix products, arithmetic and copies ran while one was open for 26% of the time, Pallas kernels for 0%

commit v1 on v0

--- a/solution.py
+++ b/solution.py
@@ -6,6 +6,22 @@
 HEADS = 12
 SEG_DEV = 2
 NEG_BIG = -1e30
+
+
+def collect(x, axis, dim):
+    ways, here, step = (lax.axis_size(axis), lax.axis_index(axis), x.shape[dim])
+    shape = [n * ways if d == dim else n for d, n in enumerate(x.shape)]
+    full = lax.dynamic_update_slice_in_dim(jnp.zeros(shape, x.dtype), x, here * step, axis=dim)
+    going_up = going_down = x
+    for far in range(1, ways // 2 + 1):
+        going_up = lax.ppermute(going_up, axis, [(d, (d + 1) % ways) for d in range(ways)])
+        full = lax.dynamic_update_slice_in_dim(full, going_up, (here - far) % ways * step, axis=dim)
+        if 2 * far < ways:
+            going_down = lax.ppermute(going_down, axis, [(d, (d - 1) % ways) for d in range(ways)])
+            full = lax.dynamic_update_slice_in_dim(
+                full, going_down, (here + far) % ways * step, axis=dim
+            )
+    return full
 
 
 def contract_last(left, right):
@@ -34,7 +50,7 @@
     per_segment = seq_count * capacity
     full_query, full_key, full_value, full_out = (
         lax.all_gather(w_query, "seq", axis=0, tiled=True),
-        lax.all_gather(w_key, "seq", axis=0, tiled=True),
+        collect(w_key, "seq", 0),
         lax.all_gather(w_value, "seq", axis=0, tiled=True),
         lax.all_gather(w_out, "seq", axis=0, tiled=True),
     )

time: 331 us -> 307 us (0.927)
  waiting for transfers between devices: 175 us -> 145 us
  starting transfers between devices: 20.3 us -> 27.7 us
    all_gather x1 -> x0, waiting for transfers between devices: 23.7 us -> none  [local(): lax.all_gather(w_key, 'seq', axis=0, tiled=True)]
    ppermute x0 -> x7, waiting for transfers between devices: none -> 13.9 us  [the longest x4 13.2 us: collect(): lax.ppermute(going_up, axis, [(d, (d + 1) % ways) for d in range(ways)])]
    all_gather x1, waiting for transfers between devices: 13.1 us -> 0.02 us  [local(): lax.all_gather(w_query, 'seq', axis=0, tiled=True)]
    ppermute x0 -> x7, starting transfers between devices: none -> 9.05 us  [the longest x3 7.95 us: collect(): lax.ppermute(going_down, axis, [(d, (d - 1) % ways) for d in range(ways)])]
    all_gather x1, waiting for transfers between devices: 15.2 us -> 8.85 us  [local(): lax.all_gather(w_value, 'seq', axis=0, tiled=True)]
    unnamed x7 -> x6, waiting for transfers between devices: 39 us -> 37.9 us
    unnamed x36 -> x38, local copies, waits for them, and re-layouts: 11.5 us -> 11.5 us
  transfers between devices with their start and end apart: 11 -> 17, of which waited for: 9 -> 11; matrix products, arithmetic and copies ran while one was open for 26% -> 28% of each run, Pallas kernels for 0% -> 0%
where the time goes in v1:
time: 307 us; the launch traced here: 304 us
  waiting for transfers between devices  145 us (47%)
  matrix products  56.5 us (18%)
  local copies, waits for them, and re-layouts  47.5 us (15%)
  starting transfers between devices  27.7 us (9%)
  between operations  15.2 us (5%)
  other arithmetic  11.8 us (4%)
    unnamed x6, waiting for transfers between devices  37.9 us
    psum x1, waiting for transfers between devices, local(): lax.psum(grad_part.astype(jnp.bfloat16), 'dp').astype(jnp.float32)  34.9 us
    all_gather x1, waiting for transfers between devices, local(): lax.all_gather(w_out, 'seq', axis=0, tiled=True)  24.1 us
    all_to_all x1, waiting for transfers between devices, local(): lax.all_to_all(send_bulk.astype(jnp.float32), 'seq', split_axis=0, concat...  21.1 us
    dot_general x12, matrix products, local_apply(): near_out = jnp.dot(weights, value_one, preferred_element_type=jnp.float32)  18.8 us
    dot_general x25, matrix products, contract_last(): lax.dot_general(left, right, (((1,), (1,)), ((), ())), preferred_element_...  17.2 us
    ppermute x4, waiting for transfers between devices, collect(): lax.ppermute(going_up, axis, [(d, (d + 1) % ways) for d in range(ways)])  13.2 us
    dot_general x14, matrix products, contract_first(): lax.dot_general(left, right, (((0,), (0,)), ((), ())), preferred_element_...  12.7 us
  transfers between devices with their start and end apart: 17, of which 11 were waited for; matrix products, arithmetic and copies ran while one was open for 28% of the time, Pallas kernels for 0%

profile of v1, /device:TPU:0, one launch (start us, length us, event | category | flops | bytes accessed | tf_op | source)
XLA Modules:
  0.0 304.2 jit_solution(9961045697008506298)
XLA Ops:
  8.5 2.9 collective-permute-start.1
  16.5 2.5 gather_fusion.1
  19.7 3.5 %all-to-all-start.1 = ((s32[8,2,20]{2,1,0:T(2,128)}), s32[8,2,20]{2,1,0:T(2,128)S(1)}, u32[]{:S(2)}, u32[]{:S(2)}) async-start(s32[8,2,20]{2,1,0:T(2,128)} %broadcast_select_fusion.2), calls=%async_computation.1 | async-start | bytes 16384 | tf_op jit(solution)/shard_map/all_to_all | solution.py:119
  24.8 2.2 collective-permute-start.3
  27.1 2.7 collective-permute-done.2
  30.6 2.8 collective-permute-start.5
  33.4 5.1 %collective-permute-done.4 = bf16[96,768]{1,0:T(8,128)(2,1)S(1)} collective-permute-done((bf16[96,768]{1,0:T(8,128)(2,1)S(1)}, bf16[96,768]{1,0:T(8,128)(2,1)S(1)}, u32[]{:S(2)}, u32[]{:S(2)}) %collective-permute-start.4) | collective-permute-done | bytes 147488 | tf_op jit(solution)/shard_map/ppermute | solution.py:17
  38.5 5.4 %collective-permute-done.6 = bf16[96,768]{1,0:T(8,128)(2,1)S(1)} collective-permute-done((bf16[96,768]{1,0:T(8,128)(2,1)S(1)}, bf16[96,768]{1,0:T(8,128)(2,1)S(1)}, u32[]{:S(2)}, u32[]{:S(2)}) %collective-permute-start.6) | collective-permute-done | bytes 147488 | tf_op jit(solution)/shard_map/ppermute | solution.py:17
  47.0 4.8 %while.41 = (s32[]{:T(128)}, f32[12,192]{1,0:T(8,128)S(1)}, f32[12,192]{1,0:T(8,128)S(1)}, bf16[12,192,64]{2,1,0:T(8,128)(2,1)S(1)}, bf16[12,192,64]{2,1,0:T(8,1...) while((s32[]{:T(128)}, f32[12,192]{1,0:T(8,128)S(1)}, ...), condition=%wide.region_7.8_spmd.clone, body=%wide.region_4.7_spmd.clone.sunk | while | flops 4976258 | bytes 400221 | solution.py:87
  52.9 2.0 gather_fusion.2
  55.4 8.8 %all-gather.6.cloned.1.call-done = bf16[768,768]{1,0:T(8,128)(2,1)} async-done(((bf16[96,768]{1,0:T(8,128)(2,1)}), bf16[768,768]{1,0:T(8,128)(2,1)}) %all-gather.6.cloned.1.call-update) | async-done | bytes 1179664 | tf_op jit(solution)/shard_map/all_gather | solution.py:54
  66.0 24.1 %all-gather.8.cloned.1.call-done = bf16[768,768]{1,0:T(8,128)(2,1)} async-done(((bf16[96,768]{1,0:T(8,128)(2,1)}), bf16[768,768]{1,0:T(8,128)(2,1)}) %all-gather.8.cloned.1.call-update) | async-done | bytes 1179664 | tf_op jit(solution)/shard_map/all_gather | solution.py:55
  90.1 1.8 convolution_convert_fusion.4
  95.1 3.9 %gather_fusion = bf16[320,4,768]{2,1,0:T(4,128)(2,1)S(1)} fusion(bf16[193,4,768]{2,1,0:T(4,128)(2,1)S(1)} %concatenate.16.clone, s32[1024]{0:T(1024)S(1)} %pad_clamp_fusion.1), kind=kCustom, calls=%fused_computation | custom fusion | bytes 3933440 | tf_op jit(solution)/shard_map/jit(_take)/gather | solution.py:102
  99.1 3.3 %all-to-all-start.2 = ((f32[8,1,960]{2,1,0:T(1,128)}), f32[8,1,960]{2,1,0:T(1,128)S(1)}, u32[]{:S(2)}, u32[]{:S(2)}) async-start(f32[8,1,960]{2,1,0:T(1,128)} %reshape.247), calls=%async_computation.2 | async-start | bytes 65536 | tf_op jit(solution)/shard_map/all_to_all | solution.py:118
  102.4 2.1 select_convert_fusion
  104.5 2.7 all-to-all-done.2
  107.2 3.8 %all-to-all-start = ((bf16[8,2,20,4,768]{4,3,2,1,0:T(4,128)(2,1)}), bf16[8,2,20,4,768]{4,3,2,1,0:T(4,128)(2,1)S(1)}, u32[]{:S(2)}, u32[]{:S(2)}) async-start(bf16[8,2,20,4,768]{4,3,2,1,0:T(4,128)(2,1)} %select_convert_fusion), calls=%async_computation | async-start | bytes 3932160 | tf_op jit(solution)/shard_map/all_to_all | solution.py:115
  114.8 21.1 %all-to-all-done = bf16[8,2,20,4,768]{4,3,2,1,0:T(4,128)(2,1)S(1)} async-done(((bf16[8,2,20,4,768]{4,3,2,1,0:T(4,128)(2,1)}), bf16[8,2,20,4,768]{4,3,2,1,0:T(4,128)(2,1)S(1)}, u32[]{:S(2)}, u32[]{:S(2)}) %all-to-all-start) | async-done | bytes 1966112 | tf_op jit(solution)/shard_map/all_to_all | solution.py:115
  135.9 2.0 copy.124
  137.9 11.5 %while.42 = (s32[]{:T(128)}, bf16[2,160,768]{2,1,0:T(8,128)(2,1)}, bf16[2,160,768]{2,1,0:T(8,128)(2,1)}, f32[2,160,12]{1,2,0:T(8,128)S(1)}, bf16[2,160,4,768]{3,...) while((s32[]{:T(128)}, bf16[2,160,768]{2,1,0:T(8,128)(2,1)}, ...), condition=%wide.region_11.12_spmd.clone, body=%wide.region_8.11_spmd.clone.sunk | while | flops 121049760 | bytes 14496293 | solution.py:150
  150.4 3.3 %all-to-all-start.3 = ((f32[8,1,480]{2,1,0:T(1,128)}), f32[8,1,480]{2,1,0:T(1,128)S(1)}, u32[]{:S(2)}, u32[]{:S(2)}) async-start(f32[8,1,480]{2,1,0:T(1,128)} %reshape.249), calls=%async_computation.3 | async-start | bytes 32768 | tf_op jit(solution)/shard_map/all_to_all | solution.py:157
  155.0 2.0 copy.147
  158.4 4.2 %all-to-all-start.4 = ((bf16[1,2,160,2,768]{4,3,1,0,2:T(2,128)(2,1)}), bf16[1,2,160,2,768]{4,3,1,0,2:T(2,128)(2,1)}, u32[]{:S(2)}, u32[]{:S(2)}) async-start(bf16[1,2,160,2,768]{4,3,1,0,2:T(2,128)(2,1)} %copy.147), calls=%async_computation.4 | async-start | bytes 1966080 | tf_op jit(solution)/shard_map/all_to_all | solution.py:154
  165.3 42.4 %while.43 = (s32[]{:T(128)}, f32[12,192,64]{1,2,0:T(8,128)}, bf16[12,192,64]{1,2,0:T(8,128)(2,1)S(1)}, bf16[12,192,64]{2,1,0:T(8,128)(2,1)}, bf16[12,192,64]{2,1...) while((s32[]{:T(128)}, f32[12,192,64]{1,2,0:T(8,128)}, ...), condition=%wide.region_13.14_spmd.clone, body=%wide.region_12.13_spmd.clone.sunk | while | flops 14376962 | bytes 546345 | solution.py:170
  208.2 1.9 copy.148
  211.7 3.1 %gather_fusion.4 = bf16[192,2,768]{2,1,0:T(2,128)(2,1)S(1)} fusion(bf16[320,2,768]{2,1,0:T(2,128)(2,1)} %bitcast.319, s32[1024]{0:T(1024)S(1)} %pad_clamp_fusion), kind=kCustom, calls=%fused_computation.4 | custom fusion | bytes 1180416 | tf_op jit(solution)/shard_map/jit(_take)/gather | solution.py:159
  217.8 2.4 copy.157
  221.7 36.4 %reduce-scatter.4.cloned.1.call-done = bf16[96,768]{1,0:T(8,128)(2,1)} async-done(((bf16[768,768]{1,0:T(8,128)(2,1)}), bf16[96,768]{1,0:T(8,128)(2,1)}) %reduce-scatter.4.cloned.1.call-update) | async-done | bytes 147472
  258.2 1.7 copy.158
  261.1 34.9 %all-reduce.5.cloned.1.call-done = bf16[96,768]{0,1:T(8,128)(2,1)} async-done(((bf16[96,768]{0,1:T(8,128)(2,1)}), bf16[96,768]{0,1:T(8,128)(2,1)}) %all-reduce.5.cloned.1.call-update) | async-done | bytes 147472 | tf_op jit(solution)/shard_map/psum | solution.py:190
  295.9 1.8 copy.151
  (259 shorter events, 93.8 us)
Async XLA Ops:
  7.2 36.8 %copy-start = (bf16[1,192,768]{2,1,0:T(8,128)(2,1)S(1)}, bf16[1,192,768]{2,1,0:T(8,128)(2,1)}, u32[]{:S(2)}) copy-start(bf16[1,192,768]{2,1,0:T(8,128)(2,1)} %param.14) | copy-start | bytes 884740
  7.2 37.7 %all-gather.4.cloned.1.call-start = ((), (), s32[]{:S(2)}) async-start(), calls=%async_computation.6 | async-start | bytes 1327104 | tf_op jit(solution)/shard_map/all_gather | solution.py:52
  7.9 56.3 %all-gather.6.cloned.1.call-start = ((), (), s32[]{:S(2)}) async-start(), calls=%async_computation.7 | async-start | bytes 1327104 | tf_op jit(solution)/shard_map/all_gather | solution.py:54
  8.0 16.3 %collective-permute-start = (bf16[96,768]{1,0:T(8,128)(2,1)}, bf16[96,768]{1,0:T(8,128)(2,1)S(1)}, u32[]{:S(2)}, u32[]{:S(2)}) collective-permute-start(bf16[96,768]{1,0:T(8,128)(2,1)} %param.19), channel_id=1, source_target_pairs={{0,1},{1,2},{2,3},{3,4},{4,5},{5,6},{6,7},{7,0},{8,9},{9,10},{10,1... | collective-permute-start | bytes 442376 | tf_op jit(solution)/shard_map/ppermute | solution.py:17
  8.5 16.3 %collective-permute-start.1 = (bf16[96,768]{1,0:T(8,128)(2,1)}, bf16[96,768]{1,0:T(8,128)(2,1)S(1)}, u32[]{:S(2)}, u32[]{:S(2)}) collective-permute-start(bf16[96,768]{1,0:T(8,128)(2,1)} %param.19), channel_id=1, source_target_pairs={{0,7},{1,0},{2,1},{3,2},{4,3},{5,4},{6,5},{7,6},{8,15},{9,8},{10,9... | collective-permute-start | bytes 442376 | tf_op jit(solution)/shard_map/ppermute | solution.py:20
  19.0 5.3 %copy-start.10 = (bf16[96,768]{1,0:T(8,128)(2,1)S(1)}, bf16[96,768]{1,0:T(8,128)(2,1)}, u32[]{:S(2)}) copy-start(bf16[96,768]{1,0:T(8,128)(2,1)} %param.19) | copy-start | bytes 442372
  19.7 79.3 %all-to-all-start.1 = ((s32[8,2,20]{2,1,0:T(2,128)}), s32[8,2,20]{2,1,0:T(2,128)S(1)}, u32[]{:S(2)}, u32[]{:S(2)}) async-start(s32[8,2,20]{2,1,0:T(2,128)} %broadcast_select_fusion.2), calls=%async_computation.1 | async-start | bytes 16384 | tf_op jit(solution)/shard_map/all_to_all | solution.py:119
  23.2 66.9 %all-gather.8.cloned.1.call-start = ((), (), s32[]{:S(2)}) async-start(), calls=%async_computation.8 | async-start | bytes 1327104 | tf_op jit(solution)/shard_map/all_gather | solution.py:55
  24.3 5.5 %collective-permute-start.2 = (bf16[96,768]{1,0:T(8,128)(2,1)S(1)}, bf16[96,768]{1,0:T(8,128)(2,1)S(1)}, u32[]{:S(2)}, u32[]{:S(2)}) collective-permute-start(bf16[96,768]{1,0:T(8,128)(2,1)S(1)} %collective-permute-done), channel_id=1, source_target_pairs={{0,1},{1,2},{2,3},{3,4},{4,5},{5,6},{6,7},{7,0},{8,9},{9,10},{10,1... | collective-permute-start | bytes 442376 | tf_op jit(solution)/shard_map/ppermute | solution.py:17
  24.8 5.7 %collective-permute-start.3 = (bf16[96,768]{1,0:T(8,128)(2,1)S(1)}, bf16[96,768]{1,0:T(8,128)(2,1)S(1)}, u32[]{:S(2)}, u32[]{:S(2)}) collective-permute-start(bf16[96,768]{1,0:T(8,128)(2,1)S(1)} %collective-permute-done.1), channel_id=1, source_target_pairs={{0,7},{1,0},{2,1},{3,2},{4,3},{5,4},{6,5},{7,6},{8,15},{9,8},{10,9... | collective-permute-start | bytes 442376 | tf_op jit(solution)/shard_map/ppermute | solution.py:20
  29.8 8.6 %collective-permute-start.4 = (bf16[96,768]{1,0:T(8,128)(2,1)S(1)}, bf16[96,768]{1,0:T(8,128)(2,1)S(1)}, u32[]{:S(2)}, u32[]{:S(2)}) collective-permute-start(bf16[96,768]{1,0:T(8,128)(2,1)S(1)} %collective-permute-done.2), channel_id=1, source_target_pairs={{0,1},{1,2},{2,3},{3,4},{4,5},{5,6},{6,7},{7,0},{8,9},{9,10},{10,1... | collective-permute-start | bytes 442376 | tf_op jit(solution)/shard_map/ppermute | solution.py:17
  30.6 7.9 %collective-permute-start.5 = (bf16[96,768]{1,0:T(8,128)(2,1)S(1)}, bf16[96,768]{1,0:T(8,128)(2,1)S(1)}, u32[]{:S(2)}, u32[]{:S(2)}) collective-permute-start(bf16[96,768]{1,0:T(8,128)(2,1)S(1)} %collective-permute-done.3), channel_id=1, source_target_pairs={{0,7},{1,0},{2,1},{3,2},{4,3},{5,4},{6,5},{7,6},{8,15},{9,8},{10,9... | collective-permute-start | bytes 442376 | tf_op jit(solution)/shard_map/ppermute | solution.py:20
  38.5 5.5 %collective-permute-start.6 = (bf16[96,768]{1,0:T(8,128)(2,1)S(1)}, bf16[96,768]{1,0:T(8,128)(2,1)S(1)}, u32[]{:S(2)}, u32[]{:S(2)}) collective-permute-start(bf16[96,768]{1,0:T(8,128)(2,1)S(1)} %collective-permute-done.4), channel_id=1, source_target_pairs={{0,1},{1,2},{2,3},{3,4},{4,5},{5,6},{6,7},{7,0},{8,9},{9,10},{10,1... | collective-permute-start | bytes 442376 | tf_op jit(solution)/shard_map/ppermute | solution.py:17
  51.9 0.8 copy-start.6
  51.9 3.1 %copy-start.7 = (bf16[12,192,64]{2,1,0:T(8,128)(2,1)}, bf16[12,192,64]{2,1,0:T(8,128)(2,1)S(1)}, u32[]{:S(2)}) copy-start(bf16[12,192,64]{2,1,0:T(8,128)(2,1)S(1)} %get-tuple-element.598) | copy-start | bytes 884740
  55.3 34.8 %copy-start.9 = (bf16[1,192,768]{2,1,0:T(8,128)(2,1)S(1)}, bf16[1,192,768]{2,1,0:T(8,128)(2,1)}, u32[]{:S(2)}) copy-start(bf16[1,192,768]{2,1,0:T(8,128)(2,1)} %param.15) | copy-start | bytes 884740
  65.9 26.9 %copy-start.2 = (bf16[192,768]{1,0:T(8,128)(2,1)}, bf16[192,768]{1,0:T(8,128)(2,1)S(1)}, u32[]{:S(2)}) copy-start(bf16[192,768]{1,0:T(8,128)(2,1)S(1)} %convolution_convert_fusion.5) | copy-start | bytes 884740
  91.9 0.7 copy-start.4
  99.1 8.1 %all-to-all-start.2 = ((f32[8,1,960]{2,1,0:T(1,128)}), f32[8,1,960]{2,1,0:T(1,128)S(1)}, u32[]{:S(2)}, u32[]{:S(2)}) async-start(f32[8,1,960]{2,1,0:T(1,128)} %reshape.247), calls=%async_computation.2 | async-start | bytes 65536 | tf_op jit(solution)/shard_map/all_to_all | solution.py:118
  104.5 6.5 %copy-start.11 = (s32[1,192,1]{1,2,0:T(1,128)S(1)}, s32[1,192,1]{1,2,0:T(1,128)}, u32[]{:S(2)}) copy-start(s32[1,192,1]{1,2,0:T(1,128)} %param.16) | copy-start | bytes 2308
  104.5 6.6 %copy-start.5 = (bf16[192,768]{1,0:T(8,128)(2,1)S(1)}, bf16[192,768]{1,0:T(8,128)(2,1)}, u32[]{:S(2)}) copy-start(bf16[192,768]{1,0:T(8,128)(2,1)} %copy-done.4) | copy-start | bytes 884740
  104.5 7.6 %copy-start.3 = (bf16[192,768]{1,0:T(8,128)(2,1)S(1)}, bf16[192,768]{1,0:T(8,128)(2,1)}, u32[]{:S(2)}) copy-start(bf16[192,768]{1,0:T(8,128)(2,1)} %copy-done.2) | copy-start | bytes 884740
  107.2 28.7 %all-to-all-start = ((bf16[8,2,20,4,768]{4,3,2,1,0:T(4,128)(2,1)}), bf16[8,2,20,4,768]{4,3,2,1,0:T(4,128)(2,1)S(1)}, u32[]{:S(2)}, u32[]{:S(2)}) async-start(bf16[8,2,20,4,768]{4,3,2,1,0:T(4,128)(2,1)} %select_convert_fusion), calls=%async_computation | async-start | bytes 3932160 | tf_op jit(solution)/shard_map/all_to_all | solution.py:115
  150.4 8.0 %all-to-all-start.3 = ((f32[8,1,480]{2,1,0:T(1,128)}), f32[8,1,480]{2,1,0:T(1,128)S(1)}, u32[]{:S(2)}, u32[]{:S(2)}) async-start(f32[8,1,480]{2,1,0:T(1,128)} %reshape.249), calls=%async_computation.3 | async-start | bytes 32768 | tf_op jit(solution)/shard_map/all_to_all | solution.py:157
  158.4 49.8 %all-to-all-start.4 = ((bf16[1,2,160,2,768]{4,3,1,0,2:T(2,128)(2,1)}), bf16[1,2,160,2,768]{4,3,1,0,2:T(2,128)(2,1)}, u32[]{:S(2)}, u32[]{:S(2)}) async-start(bf16[1,2,160,2,768]{4,3,1,0,2:T(2,128)(2,1)} %copy.147), calls=%async_computation.4 | async-start | bytes 1966080 | tf_op jit(solution)/shard_map/all_to_all | solution.py:154
  162.7 2.7 copy-start.8
  162.7 95.5 %reduce-scatter.4.cloned.1.call-start = ((), (), s32[]{:S(2)}) async-start(), calls=%async_computation.10 | async-start | bytes 1327104
  220.2 39.7 %copy-start.1 = (bf16[768,768]{1,0:T(8,128)(2,1)S(1)}, bf16[768,768]{1,0:T(8,128)(2,1)}, u32[]{:S(2)}) copy-start(bf16[768,768]{1,0:T(8,128)(2,1)} %all-gather.8.cloned.1.call-done) | copy-start | bytes 3538948
  220.2 75.7 %all-reduce.5.cloned.1.call-start = ((), (), s32[]{:S(2)}) async-start(), calls=%async_computation.9 | async-start | bytes 393216 | tf_op jit(solution)/shard_map/psum | solution.py:190
Sparse Core Ops, SparseCore 0:
  9.9 27.3 all-gather.3
  39.1 25.0 all-gather.5
  66.2 23.9 all-gather.7
  220.3 37.8 reduce-scatter.3
  260.9 34.9 all-reduce.4
